TPU v7x, 32 devices: a whole 2x2x4 slice. The times are simulated.
32 devices in a mesh: expert: 8 (over z, x), tensor: 4 (over y, core).
Axes of the slice: x: 2, y: 2, z: 4, core: 2. Of those that a mesh axis runs over, the one named last changes fastest.
Arguments:
- tokens: bfloat16 [1024, 4096], P('expert', 'tensor'), may hold values from -6 to 6
- expert_ids: int32 [1024, 8], P('expert'), may hold values from 0 to 15, all different within a row; in each aligned block of 128 rows (0 to 127, 128 to 255, ...) at most 96 rows name the same one
- combine_weight: float32 [1024, 8], P('expert'), may hold values from 0.05 to 0.5
- gate_weight: bfloat16 [16, 4096, 1024], P('expert', 'tensor'), may hold values from -0.09375 to 0.09375
- up_weight: bfloat16 [16, 4096, 1024], P('expert', 'tensor'), may hold values from -0.09375 to 0.09375
- down_weight: bfloat16 [16, 1024, 4096], P('expert', None, 'tensor'), may hold values from -0.1875 to 0.1875
- out_cotangent: bfloat16 [1024, 4096], P('expert', 'tensor'), may hold values from -3 to 3
Outputs:
- mixed: bfloat16 [1024, 4096], P('expert', 'tensor')
- token_grad: bfloat16 [1024, 4096], P('expert', 'tensor')
- combine_grad: float32 [1024, 8], P('expert')
- gate_grad: bfloat16 [16, 4096, 1024], P('expert', 'tensor')
- up_grad: bfloat16 [16, 4096, 1024], P('expert', 'tensor')
- down_grad: bfloat16 [16, 1024, 4096], P('expert', None, 'tensor')
Inputs may be any that keep to these rules, and one draw needn't show every extreme that they name: `expert_ids`: each row names 8 different experts. Among the rows of one device no expert is named by more than 96 rows, a bound that some block reaches.
All inputs are finite; a program needn't handle non-finite values.
Results may differ from a plain program's by a relative error of at most 0.023.
Values may be sent and summed in bfloat16 or wider, within the bound.
A program may use at most 128 MiB of HBM per device.

v0:
```python
import jax
import jax.numpy as jnp
from jax import lax
from jax.sharding import PartitionSpec as P


def per_device(
    tokens, expert_ids, combine_weight, gate_weight, up_weight, down_weight, out_cotangent
):
    groups = lax.axis_size("expert")
    local_experts = gate_weight.shape[0]
    width_share = tokens.shape[1]
    hidden = gate_weight.shape[2]
    tok_rows = tokens.shape[0]
    top_count = expert_ids.shape[1]
    experts_all = local_experts * groups
    capacity = 3 * tok_rows * top_count // (2 * experts_all)
    pair_count = tok_rows * top_count
    slot_total = local_experts * groups * capacity
    share_rows = hidden // lax.axis_size("tensor")
    flat_ids = expert_ids.reshape(pair_count)
    onehot = (flat_ids[:, None] == jnp.arange(experts_all, dtype=jnp.int32)[None, :]).astype(
        jnp.int32
    )
    running = jnp.cumsum(onehot, axis=0)
    position = jnp.sum(running * onehot, axis=1) - 1
    slot_of_pair = flat_ids * capacity + position
    slot_pair = (
        jnp.full((experts_all * capacity,), pair_count, jnp.int32)
        .at[slot_of_pair]
        .set(jnp.arange(pair_count, dtype=jnp.int32))
    )
    filled = slot_pair < pair_count
    safe_pair = jnp.minimum(slot_pair, pair_count - 1)
    slot_token = safe_pair // top_count
    token_send = jnp.where(filled[:, None], tokens[slot_token], jnp.zeros((), jnp.bfloat16))
    token_send = token_send.reshape(groups, local_experts * capacity, width_share)
    slot_weight = jnp.where(filled, combine_weight.reshape(pair_count)[safe_pair], jnp.float32(0.0))
    grads_send = (slot_weight[:, None] * out_cotangent[slot_token].astype(jnp.float32)).astype(
        jnp.bfloat16
    )
    grads_send = grads_send.reshape(groups, local_experts * capacity, width_share)
    routed_raw = lax.all_to_all(token_send, "expert", split_axis=0, concat_axis=0, tiled=True)
    routed = routed_raw.reshape(groups, local_experts, capacity, width_share)
    gate_part = jnp.einsum(
        "secd,edk->kesc", routed, gate_weight, preferred_element_type=jnp.float32
    ).reshape(hidden, slot_total)
    up_part = jnp.einsum(
        "secd,edk->kesc", routed, up_weight, preferred_element_type=jnp.float32
    ).reshape(hidden, slot_total)
    totals = lax.psum(
        jnp.concatenate([gate_part, up_part], axis=1).astype(jnp.bfloat16), "tensor"
    ).astype(jnp.float32)
    gate_full = totals[:, :slot_total].reshape(hidden, local_experts, groups, capacity)
    up_full = totals[:, slot_total:].reshape(hidden, local_experts, groups, capacity)
    hidden_all = (jax.nn.silu(gate_full) * up_full).astype(jnp.bfloat16)
    own_rows = lax.dynamic_slice_in_dim(
        totals, lax.axis_index("tensor") * share_rows, share_rows, 0
    )
    gate_own = own_rows[:, :slot_total].reshape(share_rows, local_experts, groups, capacity)
    up_own = own_rows[:, slot_total:].reshape(share_rows, local_experts, groups, capacity)
    expert_out = jnp.einsum(
        "fesc,efd->secd", hidden_all, down_weight, preferred_element_type=jnp.float32
    ).astype(jnp.bfloat16)
    expert_out = expert_out.reshape(groups, local_experts * capacity, width_share)
    returned = lax.all_to_all(
        expert_out, "expert", split_axis=0, concat_axis=0, tiled=True
    ).reshape(experts_all * capacity, width_share)
    pair_out = returned[slot_of_pair].reshape(tok_rows, top_count, width_share).astype(jnp.float32)
    mixed = jnp.sum(pair_out * combine_weight[:, :, None], axis=1).astype(jnp.bfloat16)
    partial_dots = jnp.sum(pair_out * out_cotangent.astype(jnp.float32)[:, None, :], axis=2)
    combine_grad = lax.psum(partial_dots, "tensor")
    grads_raw = lax.all_to_all(grads_send, "expert", split_axis=0, concat_axis=0, tiled=True)
    incoming_gradient = grads_raw.reshape(groups, local_experts, capacity, width_share)
    hidden_state_cotangent = lax.psum_scatter(
        jnp.einsum(
            "secd,ekd->kesc", incoming_gradient, down_weight, preferred_element_type=jnp.float32
        )
        .reshape(lax.axis_size("tensor") * share_rows, slot_total)
        .astype(jnp.bfloat16),
        "tensor",
        scatter_dimension=0,
        tiled=True,
    ).astype(jnp.float32)
    hidden_state_cotangent = hidden_state_cotangent.reshape(
        share_rows, local_experts, groups, capacity
    )
    down_grad = jnp.einsum(
        "fesc,secd->efd", hidden_all, incoming_gradient, preferred_element_type=jnp.float32
    ).astype(jnp.bfloat16)
    sigma = jax.nn.sigmoid(gate_own)
    gate_diff = (hidden_state_cotangent * up_own * sigma * (1.0 + gate_own * (1.0 - sigma))).astype(
        jnp.bfloat16
    )
    up_diff = (hidden_state_cotangent * jax.nn.silu(gate_own)).astype(jnp.bfloat16)
    gate_diffs, up_diffs = (
        lax.all_gather(gate_diff, "tensor", axis=0, tiled=True),
        lax.all_gather(up_diff, "tensor", axis=0, tiled=True),
    )
    routed_grad = jnp.einsum(
        "fesc,edf->secd", gate_diffs, gate_weight, preferred_element_type=jnp.float32
    )
    routed_grad = routed_grad + jnp.einsum(
        "fesc,edf->secd", up_diffs, up_weight, preferred_element_type=jnp.float32
    )
    routed_grad = routed_grad.astype(jnp.bfloat16).reshape(
        groups, local_experts * capacity, width_share
    )
    grad_back = lax.all_to_all(
        routed_grad, "expert", split_axis=0, concat_axis=0, tiled=True
    ).reshape(experts_all * capacity, width_share)
    token_grad = jnp.sum(
        grad_back[slot_of_pair].reshape(tok_rows, top_count, width_share).astype(jnp.float32),
        axis=1,
    ).astype(jnp.bfloat16)
    gate_grad = jnp.einsum(
        "secd,fesc->edf", routed, gate_diffs, preferred_element_type=jnp.float32
    ).astype(jnp.bfloat16)
    up_grad = jnp.einsum(
        "secd,fesc->edf", routed, up_diffs, preferred_element_type=jnp.float32
    ).astype(jnp.bfloat16)
    return (mixed, token_grad, combine_grad, gate_grad, up_grad, down_grad)


def solution(mesh):
    placed = (
        P("expert", "tensor"),
        P("expert", None),
        P("expert", None),
        P("expert", "tensor", None),
        P("expert", "tensor", None),
        P("expert", None, "tensor"),
        P("expert", "tensor"),
    )
    return jax.shard_map(
        per_device,
        mesh=mesh,
        in_specs=placed,
        out_specs=(
            P("expert", "tensor"),
            P("expert", "tensor"),
            P("expert", None),
            P("expert", "tensor", None),
            P("expert", "tensor", None),
            P("expert", None, "tensor"),
        ),
        check_vma=False,
    )
```

profile of v0, /device:TPU:0, one launch (start us, length us, event | category | flops | bytes accessed | tf_op | source)
XLA Modules:
  0.0 478.2 jit_solution(15574865615111957846)
XLA Ops:
  19.3 5.9 %gather_fusion.2 = f32[1536]{0:T(1024)S(1)} fusion(f32[1024]{0:T(1024)S(1)} %reshape.156, s32[2048]{0:T(1024)S(1)} %get-tuple-element.22), kind=kCustom, calls=%fused_computation.2 | custom fusion | bytes 18432 | tf_op jit(solution)/shard_map/gather | solution.py:38
  25.3 5.1 %gather_fusion = bf16[1536,1024]{1,0:T(8,128)(2,1)S(1)} fusion(bf16[128,1024]{1,0:T(8,128)(2,1)S(1)} %copy-done, s32[2048]{0:T(1024)S(1)} %get-tuple-element.23), kind=kCustom, calls=%fused_computation | custom fusion | bytes 6297600 | tf_op jit(solution)/shard_map/gather | solution.py:36
  32.3 7.4 %all-to-all-start = ((bf16[8,192,1024]{2,1,0:T(8,128)(2,1)}), bf16[8,192,1024]{2,1,0:T(8,128)(2,1)}, u32[]{:S(2)}, u32[]{:S(2)}) async-start(bf16[8,192,1024]{2,1,0:T(8,128)(2,1)} %broadcast_select_fusion), calls=%async_computation | async-start | bytes 6291456 | tf_op jit(solution)/shard_map/all_to_all | solution.py:43
  47.1 63.4 %all-to-all-done = bf16[8,192,1024]{2,1,0:T(8,128)(2,1)} async-done(((bf16[8,192,1024]{2,1,0:T(8,128)(2,1)}), bf16[8,192,1024]{2,1,0:T(8,128)(2,1)}, u32[]{:S(2)}, u32[]{:S(2)}) %all-to-all-start) | async-done | bytes 3145760 | tf_op jit(solution)/shard_map/all_to_all | solution.py:43
  114.2 6.7 %fusion.34 = bf16[2,8,96,1024]{3,2,1,0:T(8,128)(2,1)S(1)} fusion(bf16[2,1024,1024]{2,1,0:T(8,128)(2,1)} %param.11, bf16[8,2,96,1024]{3,2,1,0:T(8,128)(2,1)} %bitcast.5), kind=kOutput, calls=%fused_computation.41 | convolution fusion | flops 3222798336 | bytes 10485760 | tf_op jit(solution)/shard_map/secd,edk->kesc/dot_general | solution.py:48
  120.9 5.5 %fusion.29 = bf16[2,8,96,1024]{3,2,1,0:T(8,128)(2,1)S(1)} fusion(bf16[2,1024,1024]{2,1,0:T(8,128)(2,1)S(1)} %copy-done.5, bf16[8,2,96,1024]{3,2,1,0:T(8,128)(2,1)} %bitcast.5), kind=kOutput, calls=%fused_computation.40 | convolution fusion | flops 3222798336 | bytes 10485760 | tf_op jit(solution)/shard_map/secd,edk->kesc/dot_general | solution.py:45
  129.9 55.1 %all-to-all-done.2 = bf16[8,192,1024]{2,1,0:T(8,128)(2,1)S(1)} async-done(((bf16[8,192,1024]{2,1,0:T(8,128)(2,1)}), bf16[8,192,1024]{2,1,0:T(8,128)(2,1)S(1)}, u32[]{:S(2)}, u32[]{:S(2)}) %all-to-all-start.2) | async-done | bytes 3145760 | tf_op jit(solution)/shard_map/all_to_all | solution.py:73
  185.0 8.2 %fusion.24 = bf16[2,8,96,1024]{3,2,1,0:T(8,128)(2,1)} fusion(bf16[2,1024,1024]{2,1,0:T(8,128)(2,1)} %param.12, bf16[8,2,96,1024]{3,2,1,0:T(8,128)(2,1)S(1)} %bitcast.103), kind=kOutput, calls=%fused_computation.39 | convolution fusion | flops 3222798336 | bytes 10485760 | tf_op jit(solution)/shard_map/secd,ekd->kesc/dot_general | solution.py:76
  193.7 57.2 %all-reduce.2.cloned.1.call-done = bf16[1024,3072]{0,1:T(8,128)(2,1)} async-done(((bf16[1024,3072]{0,1:T(8,128)(2,1)}), bf16[1024,3072]{0,1:T(8,128)(2,1)}) %all-reduce.2.cloned.1.call-update) | async-done | bytes 6291472 | tf_op jit(solution)/shard_map/psum | solution.py:51
  256.7 35.3 %reduce-scatter.2.cloned.1.call-done = bf16[256,1536]{0,1:T(8,128)(2,1)} async-done(((bf16[1024,1536]{0,1:T(8,128)(2,1)}), bf16[256,1536]{0,1:T(8,128)(2,1)}) %reduce-scatter.2.cloned.1.call-update) | async-done | bytes 786448 | tf_op jit(solution)/shard_map/reduce_scatter | solution.py:75
  301.7 7.1 %convert_bitcast_fusion = bf16[8,2,96,1024]{3,2,0,1:T(8,128)(2,1)S(1)} fusion(bf16[1024,2,8,96]{0,3,2,1:T(8,128)(2,1)S(1)} %multiply_convert_fusion, bf16[2,1024,1024]{2,1,0:T(8,128)(2,1)} %param.12), kind=kOutput, calls=%fused_computation.33 | convolution fusion | flops 3222798336 | bytes 10485760 | tf_op jit(solution)/shard_map/fesc,efd->secd/dot_general | solution.py:62
  310.8 5.8 %all-to-all-start.1 = ((bf16[8,192,1024]{2,1,0:T(8,128)(2,1)}), bf16[8,192,1024]{2,1,0:T(8,128)(2,1)S(1)}, u32[]{:S(2)}, u32[]{:S(2)}) async-start(bf16[8,192,1024]{2,1,0:T(8,128)(2,1)} %bitcast.98), calls=%async_computation.1 | async-start | bytes 6291456 | tf_op jit(solution)/shard_map/all_to_all | solution.py:66
  316.7 7.5 %all-gather.5.cloned.1.call-done = bf16[1024,2,8,96]{0,3,2,1:T(8,128)(2,1)} async-done(((bf16[256,2,8,96]{0,3,2,1:T(8,128)(2,1)}), bf16[1024,2,8,96]{0,3,2,1:T(8,128)(2,1)}) %all-gather.5.cloned.1.call-update) | async-done | bytes 3145744 | tf_op jit(solution)/shard_map/all_gather | solution.py:98
  324.2 9.4 %fusion.3 = f32[2,8,96,1024]{3,2,1,0:T(8,128)} fusion(bf16[1024,2,8,96]{0,3,2,1:T(8,128)(2,1)} %all-gather.5.cloned.1.call-done, bf16[2,1024,1024]{2,1,0:T(8,128)(2,1)} %param.11), kind=kOutput, calls=%fused_computation.18 | convolution fusion | flops 3221225472 | bytes 13631488 | tf_op jit(solution)/shard_map/fesc,edf->secd/dot_general | solution.py:103
  333.6 21.0 %all-gather.3.cloned.1.call-done = bf16[1024,2,8,96]{0,3,2,1:T(8,128)(2,1)} async-done(((bf16[256,2,8,96]{0,3,2,1:T(8,128)(2,1)}), bf16[1024,2,8,96]{0,3,2,1:T(8,128)(2,1)}) %all-gather.3.cloned.1.call-update) | async-done | bytes 3145744 | tf_op jit(solution)/shard_map/all_gather | solution.py:97
  354.6 8.4 %fusion.15 = bf16[8,2,96,1024]{3,2,0,1:T(8,128)(2,1)S(1)} fusion(f32[2,8,96,1024]{3,2,1,0:T(8,128)} %fusion.3, bf16[1024,2,8,96]{0,3,2,1:T(8,128)(2,1)} %all-gather.3.cloned.1.call-done, bf16[2,1024,1024]{2,1,0:T(8,128)(2,1)} %param.10), kind=kOutput, calls=%fused_computation.30 | convolution fusion | flops 3224371200 | bytes 16777216 | tf_op jit(solution)/shard_map/fesc,edf->secd/dot_general | solution.py:100
  364.9 22.4 %all-to-all-done.1 = bf16[8,192,1024]{2,1,0:T(8,128)(2,1)S(1)} async-done(((bf16[8,192,1024]{2,1,0:T(8,128)(2,1)}), bf16[8,192,1024]{2,1,0:T(8,128)(2,1)S(1)}, u32[]{:S(2)}, u32[]{:S(2)}) %all-to-all-start.1) | async-done | bytes 3145760 | tf_op jit(solution)/shard_map/all_to_all | solution.py:66
  392.6 8.3 %bitcast_convert_fusion = bf16[2,1024,1024]{2,1,0:T(8,128)(2,1)} fusion(bf16[1024,2,8,96]{0,3,2,1:T(8,128)(2,1)} %copy-done.4, bf16[8,2,96,1024]{3,2,1,0:T(8,128)(2,1)} %bitcast.104), kind=kOutput, calls=%fused_computation.6 | convolution fusion | flops 3223322624 | bytes 10485760 | tf_op jit(solution)/shard_map/fesc,secd->efd/dot_general | solution.py:88
  400.9 5.3 %gather_fusion.1 = bf16[1024,1024]{1,0:T(8,128)(2,1)} fusion(bf16[1536,1024]{1,0:T(8,128)(2,1)S(1)} %bitcast.94, s32[1024]{0:T(1024)S(1)} %broadcast_clamp_fusion), kind=kCustom, calls=%fused_computation.1 | custom fusion | bytes 4198400 | tf_op jit(solution)/shard_map/gather | solution.py:69
  410.5 11.7 %psum.15 = f32[128,8]{1,0:T(8,128)S(1)} all-reduce(f32[128,8]{1,0:T(8,128)S(1)} %get-tuple-element.12), channel_id=1, replica_groups=mesh['expert'=8,'tensor'=4] {'tensor'}, use_global_device_ids=true, to_apply=%region_9.10 | all-reduce | flops 1024 | bytes 8192 | tf_op jit(solution)/shard_map/psum | solution.py:72
  422.8 7.0 %bitcast_convert_fusion.1 = bf16[2,1024,1024]{2,1,0:T(8,128)(2,1)} fusion(bf16[8,2,96,1024]{3,2,1,0:T(8,128)(2,1)} %bitcast.5, bf16[1024,2,8,96]{0,3,2,1:T(8,128)(2,1)S(1)} %copy-done.6), kind=kOutput, calls=%fused_computation.7 | convolution fusion | flops 3223322624 | bytes 10485760 | tf_op jit(solution)/shard_map/secd,fesc->edf/dot_general | solution.py:119
  429.9 6.9 %bitcast_convert_fusion.2 = bf16[2,1024,1024]{2,1,0:T(8,128)(2,1)} fusion(bf16[8,2,96,1024]{3,2,1,0:T(8,128)(2,1)} %bitcast.5, bf16[1024,2,8,96]{0,3,2,1:T(8,128)(2,1)S(1)} %copy-done.7), kind=kOutput, calls=%fused_computation.8 | convolution fusion | flops 3223322624 | bytes 10485760 | tf_op jit(solution)/shard_map/secd,fesc->edf/dot_general | solution.py:116
  436.8 25.2 %all-to-all-done.3 = bf16[8,192,1024]{2,1,0:T(8,128)(2,1)} async-done(((bf16[8,192,1024]{2,1,0:T(8,128)(2,1)}), bf16[8,192,1024]{2,1,0:T(8,128)(2,1)}, u32[]{:S(2)}, u32[]{:S(2)}) %all-to-all-start.3) | async-done | bytes 3145760 | tf_op jit(solution)/shard_map/all_to_all | solution.py:109
  461.9 7.3 %gather_fusion.4 = bf16[1024,1024]{1,0:T(8,128)(2,1)S(1)} fusion(bf16[1536,1024]{1,0:T(8,128)(2,1)} %bitcast.35, s32[1024]{0:T(1024)S(1)} %broadcast_clamp_fusion), kind=kCustom, calls=%fused_computation.4 | custom fusion | bytes 4198400 | tf_op jit(solution)/shard_map/gather | solution.py:113
  (69 shorter events, 60.8 us)
Async XLA Ops:
  7.2 18.1 %copy-start = (bf16[128,1024]{1,0:T(8,128)(2,1)S(1)}, bf16[128,1024]{1,0:T(8,128)(2,1)}, u32[]{:S(2)}) copy-start(bf16[128,1024]{1,0:T(8,128)(2,1)} %param.7) | copy-start | bytes 786436
  32.3 7.5 %copy-start.2 = (bf16[128,1024]{1,0:T(8,128)(2,1)S(1)}, bf16[128,1024]{1,0:T(8,128)(2,1)}, u32[]{:S(2)}) copy-start(bf16[128,1024]{1,0:T(8,128)(2,1)} %param.13) | copy-start | bytes 786436
  32.3 78.2 %all-to-all-start = ((bf16[8,192,1024]{2,1,0:T(8,128)(2,1)}), bf16[8,192,1024]{2,1,0:T(8,128)(2,1)}, u32[]{:S(2)}, u32[]{:S(2)}) async-start(bf16[8,192,1024]{2,1,0:T(8,128)(2,1)} %broadcast_select_fusion), calls=%async_computation | async-start | bytes 6291456 | tf_op jit(solution)/shard_map/all_to_all | solution.py:43
  110.5 74.5 %all-to-all-start.2 = ((bf16[8,192,1024]{2,1,0:T(8,128)(2,1)}), bf16[8,192,1024]{2,1,0:T(8,128)(2,1)S(1)}, u32[]{:S(2)}, u32[]{:S(2)}) async-start(bf16[8,192,1024]{2,1,0:T(8,128)(2,1)} %fusion), calls=%async_computation.2 | async-start | bytes 6291456 | tf_op jit(solution)/shard_map/all_to_all | solution.py:73
  114.1 136.8 %all-reduce.2.cloned.1.call-start = ((), (), s32[]{:S(2)}) async-start(), calls=%async_computation.5 | async-start | bytes 12582912 | tf_op jit(solution)/shard_map/psum | solution.py:51
  114.2 6.7 %copy-start.5 = (bf16[2,1024,1024]{2,1,0:T(8,128)(2,1)S(1)}, bf16[2,1024,1024]{2,1,0:T(8,128)(2,1)}, u32[]{:S(2)}) copy-start(bf16[2,1024,1024]{2,1,0:T(8,128)(2,1)} %param.10) | copy-start | bytes 12582916
  129.8 162.2 %reduce-scatter.2.cloned.1.call-start = ((), (), s32[]{:S(2)}) async-start(), calls=%async_computation.6 | async-start | bytes 3932160 | tf_op jit(solution)/shard_map/reduce_scatter | solution.py:75
  185.0 8.2 %copy-start.3 = (bf16[8,192,1024]{2,1,0:T(8,128)(2,1)}, bf16[8,192,1024]{2,1,0:T(8,128)(2,1)S(1)}, u32[]{:S(2)}) copy-start(bf16[8,192,1024]{2,1,0:T(8,128)(2,1)S(1)} %all-to-all-done.2) | copy-start | bytes 9437188
  193.2 131.0 %all-gather.5.cloned.1.call-start = ((), (), s32[]{:S(2)}) async-start(), calls=%async_computation.8 | async-start | bytes 3932160 | tf_op jit(solution)/shard_map/all_gather | solution.py:98
  295.1 59.4 %all-gather.3.cloned.1.call-start = ((), (), s32[]{:S(2)}) async-start(), calls=%async_computation.7 | async-start | bytes 3932160 | tf_op jit(solution)/shard_map/all_gather | solution.py:97
  301.7 7.1 %copy-start.4 = (bf16[1024,2,8,96]{0,3,2,1:T(8,128)(2,1)}, bf16[1024,2,8,96]{0,3,2,1:T(8,128)(2,1)S(1)}, u32[]{:S(2)}) copy-start(bf16[1024,2,8,96]{0,3,2,1:T(8,128)(2,1)S(1)} %multiply_convert_fusion) | copy-start | bytes 9437188
  310.8 76.5 %all-to-all-start.1 = ((bf16[8,192,1024]{2,1,0:T(8,128)(2,1)}), bf16[8,192,1024]{2,1,0:T(8,128)(2,1)S(1)}, u32[]{:S(2)}, u32[]{:S(2)}) async-start(bf16[8,192,1024]{2,1,0:T(8,128)(2,1)} %bitcast.98), calls=%async_computation.1 | async-start | bytes 6291456 | tf_op jit(solution)/shard_map/all_to_all | solution.py:66
  387.3 74.7 %all-to-all-start.3 = ((bf16[8,192,1024]{2,1,0:T(8,128)(2,1)}), bf16[8,192,1024]{2,1,0:T(8,128)(2,1)}, u32[]{:S(2)}, u32[]{:S(2)}) async-start(bf16[8,192,1024]{2,1,0:T(8,128)(2,1)} %bitcast.97), calls=%async_computation.4 | async-start | bytes 6291456 | tf_op jit(solution)/shard_map/all_to_all | solution.py:109
  406.2 16.6 %copy-start.6 = (bf16[1024,2,8,96]{0,3,2,1:T(8,128)(2,1)S(1)}, bf16[1024,2,8,96]{0,3,2,1:T(8,128)(2,1)}, u32[]{:S(2)}) copy-start(bf16[1024,2,8,96]{0,3,2,1:T(8,128)(2,1)} %all-gather.5.cloned.1.call-done) | copy-start | bytes 9437188
  422.8 7.1 %copy-start.7 = (bf16[1024,2,8,96]{0,3,2,1:T(8,128)(2,1)S(1)}, bf16[1024,2,8,96]{0,3,2,1:T(8,128)(2,1)}, u32[]{:S(2)}) copy-start(bf16[1024,2,8,96]{0,3,2,1:T(8,128)(2,1)} %all-gather.3.cloned.1.call-done) | copy-start | bytes 9437188
  461.9 9.4 %copy-start.1 = (bf16[128,1024]{1,0:T(8,128)(2,1)S(1)}, bf16[128,1024]{1,0:T(8,128)(2,1)}, u32[]{:S(2)}) copy-start(bf16[128,1024]{1,0:T(8,128)(2,1)} %param.7) | copy-start | bytes 786436
Sparse Core Ops, SparseCore 0:
  130.0 120.9 all-reduce.1
  254.0 37.9 reduce-scatter.1
  295.3 28.9 all-gather.4
  325.6 28.8 all-gather.2
where the time goes:
time: 487 us; the launch traced here: 478 us
  waiting for transfers between devices  287 us (59%)
  matrix products  67.5 us (14%)
  local copies, waits for them, and re-layouts  46 us (9%)
  other arithmetic  29.6 us (6%)
  starting transfers between devices  22 us (5%)
  between operations  14.3 us (3%)
  blocking collectives  11.7 us (2%)
    all_to_all x1, waiting for transfers between devices, per_device(): lax.all_to_all(token_send, 'expert', split_axis=0, concat_axis=0, tiled=T...  63.4 us
    psum x1, waiting for transfers between devices, per_device(): lax.psum(jnp.concatenate([gate_part, up_part], axis=1).astype(jnp.bfloat1...  57.2 us
    all_to_all x1, waiting for transfers between devices, per_device(): lax.all_to_all(grads_send, 'expert', split_axis=0, concat_axis=0, tiled=T...  55.1 us
    reduce_scatter x1, waiting for transfers between devices, per_device(): lax.psum_scatter(jnp.einsum('secd,ekd->kesc', incoming_gradient, down_wei...  35.3 us
    all_to_all x1, waiting for transfers between devices, per_device(): lax.all_to_all(routed_grad, 'expert', split_axis=0, concat_axis=0, tiled=...  25.2 us
    all_to_all x1, waiting for transfers between devices, per_device(): lax.all_to_all(expert_out, 'expert', split_axis=0, concat_axis=0, tiled=T...  22.4 us
    all_gather x1, waiting for transfers between devices, per_device(): lax.all_gather(gate_diff, 'tensor', axis=0, tiled=True)  21 us
    psum x1, blocking collectives, per_device(): combine_grad = lax.psum(partial_dots, 'tensor')  11.7 us
  transfers between devices with their start and end apart: 8, of which 8 were waited for; matrix products, arithmetic and copies ran while one was open for 22% of the time, Pallas kernels for 0%

commit v1 on v0

--- a/solution.py
+++ b/solution.py
@@ -48,8 +48,11 @@
     up_part = jnp.einsum(
         "secd,edk->kesc", routed, up_weight, preferred_element_type=jnp.float32
     ).reshape(hidden, slot_total)
-    totals = lax.psum(
-        jnp.concatenate([gate_part, up_part], axis=1).astype(jnp.bfloat16), "tensor"
+    totals = jnp.sum(
+        lax.all_gather(
+            jnp.concatenate([gate_part, up_part], axis=1).astype(jnp.bfloat16), "tensor"
+        ),
+        axis=0,
     ).astype(jnp.float32)
     gate_full = totals[:, :slot_total].reshape(hidden, local_experts, groups, capacity)
     up_full = totals[:, slot_total:].reshape(hidden, local_experts, groups, capacity)

time: 487 us -> 544 us (1.12)
  blocking collectives: 11.7 us -> 164 us
  waiting for transfers between devices: 287 us -> 151 us
  local copies, waits for them, and re-layouts: 46 us -> 75.2 us
  other arithmetic: 29.6 us -> 51.6 us
  matrix products: 67.5 us -> 57.7 us
    all_to_all x0 -> x2, blocking collectives: none -> 152 us  [the longest x1 78 us: per_device(): lax.all_to_all(token_send, 'expert', split_axis=0, concat_axis=0, tiled=T...]
    all_to_all x2 -> x0, waiting for transfers between devices: 119 us -> none  [the longest x1 63.4 us: per_device(): lax.all_to_all(token_send, 'expert', split_axis=0, concat_axis=0, tiled=T...]
    all_gather x0 -> x1, waiting for transfers between devices: none -> 57.4 us  [per_device(): lax.all_gather(jnp.concatenate([gate_part, up_part], axis=1).astype(jnp.b...]
    psum x1 -> x0, waiting for transfers between devices: 57.2 us -> none  [per_device(): lax.psum(jnp.concatenate([gate_part, up_part], axis=1).astype(jnp.bfloat1...]
    reduce_scatter x1, waiting for transfers between devices: 35.3 us -> 13.9 us  [per_device(): lax.psum_scatter(jnp.einsum('secd,ekd->kesc', incoming_gradient, down_wei...]
    reduce_sum x0 -> x1, other arithmetic: none -> 18.5 us  [per_device(): jnp.sum(lax.all_gather(jnp.concatenate([gate_part, up_part], axis=1).asty...]
    all_to_all x1, waiting for transfers between devices: 22.4 us -> 40.5 us  [per_device(): lax.all_to_all(expert_out, 'expert', split_axis=0, concat_axis=0, tiled=T...]
    slice x1 -> x2, local copies, waits for them, and re-layouts: 4.38 us -> 16.1 us  [per_device(): totals[:, :slot_total].reshape(hidden, local_experts, groups, capacity)]
  transfers between devices with their start and end apart: 8 -> 6, of which waited for: 8 -> 5; matrix products, arithmetic and copies ran while one was open for 22% -> 23% of each run, Pallas kernels for 0% -> 0%
where the time goes in v1:
time: 544 us; the launch traced here: 535 us
  blocking collectives  164 us (30%)
  waiting for transfers between devices  151 us (28%)
  local copies, waits for them, and re-layouts  75.2 us (14%)
  matrix products  57.7 us (11%)
  other arithmetic  51.6 us (9%)
  starting transfers between devices  21.3 us (4%)
  between operations  14.4 us (3%)
    all_to_all x1, blocking collectives, per_device(): lax.all_to_all(token_send, 'expert', split_axis=0, concat_axis=0, tiled=T...  78 us
    all_to_all x1, blocking collectives, per_device(): lax.all_to_all(grads_send, 'expert', split_axis=0, concat_axis=0, tiled=T...  74.1 us
    all_gather x1, waiting for transfers between devices, per_device(): lax.all_gather(jnp.concatenate([gate_part, up_part], axis=1).astype(jnp.b...  57.4 us
    all_to_all x1, waiting for transfers between devices, per_device(): lax.all_to_all(expert_out, 'expert', split_axis=0, concat_axis=0, tiled=T...  40.5 us
    all_to_all x1, waiting for transfers between devices, per_device(): lax.all_to_all(routed_grad, 'expert', split_axis=0, concat_axis=0, tiled=...  29 us
    reduce_sum x1, other arithmetic, per_device(): jnp.sum(lax.all_gather(jnp.concatenate([gate_part, up_part], axis=1).asty...  18.5 us
    slice x2, local copies, waits for them, and re-layouts, per_device(): totals[:, :slot_total].reshape(hidden, local_experts, groups, capacity)  16.1 us
    reduce_scatter x1, waiting for transfers between devices, per_device(): lax.psum_scatter(jnp.einsum('secd,ekd->kesc', incoming_gradient, down_wei...  13.9 us
  transfers between devices with their start and end apart: 6, of which 5 were waited for; matrix products, arithmetic and copies ran while one was open for 23% of the time, Pallas kernels for 0%

profile of v1, /device:TPU:0, one launch (start us, length us, event | category | flops | bytes accessed | tf_op | source)
XLA Modules:
  0.0 535.0 jit_solution(13478847694117924862)
XLA Ops:
  19.4 5.9 %gather_fusion.2 = f32[1536]{0:T(1024)S(1)} fusion(f32[1024]{0:T(1024)S(1)} %reshape.181, s32[2048]{0:T(1024)S(1)} %get-tuple-element.34), kind=kCustom, calls=%fused_computation.2 | custom fusion | bytes 18432 | tf_op jit(solution)/shard_map/gather | solution.py:38
  25.3 5.1 gather_fusion
  30.9 78.0 %all_to_all.20 = bf16[8,192,1024]{2,1,0:T(8,128)(2,1)S(1)} all-to-all(bf16[8,192,1024]{2,1,0:T(8,128)(2,1)S(1)} %broadcast_select_fusion), channel_id=1, replica_groups=mesh['expert'=8,'tensor'=4] {'expert'}, dimensions={0} | all-to-all | bytes 6291456 | tf_op jit(solution)/shard_map/all_to_all | solution.py:43
  116.9 8.2 %fusion.34 = bf16[2,8,96,1024]{3,2,1,0:T(8,128)(2,1)} fusion(bf16[2,1024,1024]{2,1,0:T(8,128)(2,1)} %param.11, bf16[8,2,96,1024]{3,2,1,0:T(8,128)(2,1)} %bitcast.104), kind=kOutput, calls=%fused_computation.41 | convolution fusion | flops 3222798336 | bytes 10485760 | tf_op jit(solution)/shard_map/secd,edk->kesc/dot_general | solution.py:48
  129.7 5.3 pad_maximum_fusion
  141.7 74.1 %all_to_all.21 = bf16[8,192,1024]{2,1,0:T(8,128)(2,1)S(1)} all-to-all(bf16[8,192,1024]{2,1,0:T(8,128)(2,1)S(1)} %fusion), channel_id=1, replica_groups=mesh['expert'=8,'tensor'=4] {'expert'}, dimensions={0} | all-to-all | bytes 6291456 | tf_op jit(solution)/shard_map/all_to_all | solution.py:76
  220.7 11.0 %all-gather.8.cloned.1.call-start = ((), (), s32[]{:S(2)}) async-start(), calls=%async_computation.8 | async-start | bytes 3932160 | tf_op jit(solution)/shard_map/all_gather | solution.py:101
  231.6 57.4 %all-gather.4.cloned.1.call-done = bf16[4,1024,3072]{2,1,0:T(8,128)(2,1)} async-done(((bf16[1,1024,3072]{2,1,0:T(8,128)(2,1)}), bf16[4,1024,3072]{2,1,0:T(8,128)(2,1)}) %all-gather.4.cloned.1.call-update) | async-done | bytes 25165840 | tf_op jit(solution)/shard_map/all_gather | solution.py:52
  289.1 18.5 %reduce_sum.52 = bf16[1024,3072]{1,0:T(8,128)(2,1)} reduce(bf16[4,1024,3072]{2,1,0:T(8,128)(2,1)} %all-gather.4.cloned.1.call-done, bf16[]{:T(256)} %constant.49.clone.1), dimensions={0}, to_apply=%region_4.5 | reduce | flops 9437184 | bytes 31457282 | tf_op jit(solution)/shard_map/reduce_sum | solution.py:51
  316.1 13.9 %reduce-scatter.2.cloned.1.call-done = bf16[256,1536]{0,1:T(8,128)(2,1)} async-done(((bf16[1024,1536]{0,1:T(8,128)(2,1)}), bf16[256,1536]{0,1:T(8,128)(2,1)}) %reduce-scatter.2.cloned.1.call-update) | async-done | bytes 786448 | tf_op jit(solution)/shard_map/reduce_scatter | solution.py:78
  333.6 9.6 %fusion.52 = (f32[1024,1536]{1,0:T(8,128)}, f32[1024,1536]{1,0:T(8,128)}) fusion(bf16[1024,3072]{1,0:T(8,128)(2,1)} %reduce_sum.52), kind=kLoop, calls=%fused_computation.77 | loop fusion | bytes 25165824 | tf_op jit(solution)/shard_map/slice | solution.py:57
  343.1 6.6 %copy.81 = f32[1024,1536]{0,1:T(8,128)} copy(f32[1024,1536]{1,0:T(8,128)} %get-tuple-element.28) | data formatting | bytes 12582912 | tf_op jit(solution)/shard_map/slice | solution.py:57
  349.7 6.6 %copy.82 = f32[1024,1536]{0,1:T(8,128)} copy(f32[1024,1536]{1,0:T(8,128)} %get-tuple-element.29) | data formatting | bytes 12582912 | tf_op jit(solution)/shard_map/slice | solution.py:58
  356.4 5.8 %multiply_convert_fusion = bf16[1024,2,8,96]{0,3,2,1:T(8,128)(2,1)S(1)} fusion(f32[1024,2,8,96]{0,3,2,1:T(8,128)} %bitcast.96, f32[1024,2,8,96]{0,3,2,1:T(8,128)} %bitcast.95), kind=kLoop, calls=%fused_computation.13 | loop fusion | flops 9437184 | bytes 15728640 | tf_op jit(solution)/shard_map/convert_element_type | solution.py:59
  368.0 5.5 %all-to-all-start.1 = ((bf16[8,192,1024]{2,1,0:T(8,128)(2,1)}), bf16[8,192,1024]{2,1,0:T(8,128)(2,1)S(1)}, u32[]{:S(2)}, u32[]{:S(2)}) async-start(bf16[8,192,1024]{2,1,0:T(8,128)(2,1)} %bitcast.98), calls=%async_computation.1 | async-start | bytes 6291456 | tf_op jit(solution)/shard_map/all_to_all | solution.py:69
  373.5 9.4 %fusion.3 = f32[2,8,96,1024]{3,2,1,0:T(8,128)} fusion(bf16[1024,2,8,96]{0,3,2,1:T(8,128)(2,1)} %all-gather.8.cloned.1.call-done, bf16[2,1024,1024]{2,1,0:T(8,128)(2,1)} %param.11), kind=kOutput, calls=%fused_computation.18 | convolution fusion | flops 3221225472 | bytes 13631488 | tf_op jit(solution)/shard_map/fesc,edf->secd/dot_general | solution.py:106
  382.8 10.1 %all-gather.6.cloned.1.call-done = bf16[1024,2,8,96]{0,3,2,1:T(8,128)(2,1)} async-done(((bf16[256,2,8,96]{0,3,2,1:T(8,128)(2,1)}), bf16[1024,2,8,96]{0,3,2,1:T(8,128)(2,1)}) %all-gather.6.cloned.1.call-update) | async-done | bytes 3145744 | tf_op jit(solution)/shard_map/all_gather | solution.py:100
  392.9 8.4 %fusion.15 = bf16[8,2,96,1024]{3,2,0,1:T(8,128)(2,1)S(1)} fusion(f32[2,8,96,1024]{3,2,1,0:T(8,128)} %fusion.3, bf16[1024,2,8,96]{0,3,2,1:T(8,128)(2,1)} %all-gather.6.cloned.1.call-done, bf16[2,1024,1024]{2,1,0:T(8,128)(2,1)} %param.10), kind=kOutput, calls=%fused_computation.30 | convolution fusion | flops 3224371200 | bytes 16777216 | tf_op jit(solution)/shard_map/fesc,edf->secd/dot_general | solution.py:103
  403.4 40.5 %all-to-all-done.1 = bf16[8,192,1024]{2,1,0:T(8,128)(2,1)S(1)} async-done(((bf16[8,192,1024]{2,1,0:T(8,128)(2,1)}), bf16[8,192,1024]{2,1,0:T(8,128)(2,1)S(1)}, u32[]{:S(2)}, u32[]{:S(2)}) %all-to-all-start.1) | async-done | bytes 3145760 | tf_op jit(solution)/shard_map/all_to_all | solution.py:69
  449.4 8.5 %bitcast_convert_fusion = bf16[2,1024,1024]{2,1,0:T(8,128)(2,1)} fusion(bf16[1024,2,8,96]{0,3,2,1:T(8,128)(2,1)} %copy-done.6, bf16[8,2,96,1024]{3,2,1,0:T(8,128)(2,1)} %bitcast.108), kind=kOutput, calls=%fused_computation.6 | convolution fusion | flops 3223322624 | bytes 10485760 | tf_op jit(solution)/shard_map/fesc,secd->efd/dot_general | solution.py:91
  467.9 5.3 gather_fusion.1
  477.3 11.6 %psum.7 = f32[128,8]{1,0:T(8,128)S(1)} all-reduce(f32[128,8]{1,0:T(8,128)S(1)} %get-tuple-element.24), channel_id=1, replica_groups=mesh['expert'=8,'tensor'=4] {'tensor'}, use_global_device_ids=true, to_apply=%region_9.10 | all-reduce | flops 1024 | bytes 8192 | tf_op jit(solution)/shard_map/psum | solution.py:75
  489.6 29.0 %all-to-all-done.3 = bf16[8,192,1024]{2,1,0:T(8,128)(2,1)} async-done(((bf16[8,192,1024]{2,1,0:T(8,128)(2,1)}), bf16[8,192,1024]{2,1,0:T(8,128)(2,1)}, u32[]{:S(2)}, u32[]{:S(2)}) %all-to-all-start.3) | async-done | bytes 3145760 | tf_op jit(solution)/shard_map/all_to_all | solution.py:112
  518.6 7.3 %gather_fusion.4 = bf16[1024,1024]{1,0:T(8,128)(2,1)S(1)} fusion(bf16[1536,1024]{1,0:T(8,128)(2,1)} %bitcast.35, s32[1024]{0:T(1024)S(1)} %broadcast_clamp_fusion), kind=kCustom, calls=%fused_computation.4 | custom fusion | bytes 4198400 | tf_op jit(solution)/shard_map/gather | solution.py:116
  (82 shorter events, 79.0 us)
Async XLA Ops:
  7.2 18.2 %copy-start = (bf16[128,1024]{1,0:T(8,128)(2,1)S(1)}, bf16[128,1024]{1,0:T(8,128)(2,1)}, u32[]{:S(2)}) copy-start(bf16[128,1024]{1,0:T(8,128)(2,1)} %param.7) | copy-start | bytes 786436
  7.2 281.9 %all-gather.4.cloned.1.call-start = ((), (), s32[]{:S(2)}) async-start(), calls=%async_computation.5 | async-start | bytes 31457280 | tf_op jit(solution)/shard_map/all_gather | solution.py:52
  30.9 78.1 %copy-start.9 = (bf16[2,1024,1024]{2,1,0:T(8,128)(2,1)S(1)}, bf16[2,1024,1024]{2,1,0:T(8,128)(2,1)}, u32[]{:S(2)}) copy-start(bf16[2,1024,1024]{2,1,0:T(8,128)(2,1)} %param.10) | copy-start | bytes 12582916
  108.9 4.8 copy-start.3
  135.1 0.9 copy-start.2
  135.1 194.8 %reduce-scatter.2.cloned.1.call-start = ((), (), s32[]{:S(2)}) async-start(), calls=%async_computation.6 | async-start | bytes 3932160 | tf_op jit(solution)/shard_map/reduce_scatter | solution.py:78
  141.7 74.2 %copy-start.7 = (bf16[2,1024,1024]{2,1,0:T(8,128)(2,1)S(1)}, bf16[2,1024,1024]{2,1,0:T(8,128)(2,1)}, u32[]{:S(2)}) copy-start(bf16[2,1024,1024]{2,1,0:T(8,128)(2,1)} %param.12) | copy-start | bytes 12582916
  215.8 4.8 copy-start.5
  220.7 152.8 %all-gather.8.cloned.1.call-start = ((), (), s32[]{:S(2)}) async-start(), calls=%async_computation.8 | async-start | bytes 3932160 | tf_op jit(solution)/shard_map/all_gather | solution.py:101
  333.5 59.4 %all-gather.6.cloned.1.call-start = ((), (), s32[]{:S(2)}) async-start(), calls=%async_computation.7 | async-start | bytes 3932160 | tf_op jit(solution)/shard_map/all_gather | solution.py:100
  356.4 5.9 %copy-start.8 = (bf16[2,1024,1024]{2,1,0:T(8,128)(2,1)S(1)}, bf16[2,1024,1024]{2,1,0:T(8,128)(2,1)}, u32[]{:S(2)}) copy-start(bf16[2,1024,1024]{2,1,0:T(8,128)(2,1)} %param.12) | copy-start | bytes 12582916
  362.3 3.6 copy-start.6
  368.0 75.9 %all-to-all-start.1 = ((bf16[8,192,1024]{2,1,0:T(8,128)(2,1)}), bf16[8,192,1024]{2,1,0:T(8,128)(2,1)S(1)}, u32[]{:S(2)}, u32[]{:S(2)}) async-start(bf16[8,192,1024]{2,1,0:T(8,128)(2,1)} %bitcast.98), calls=%async_computation.1 | async-start | bytes 6291456 | tf_op jit(solution)/shard_map/all_to_all | solution.py:69
  443.9 74.7 %all-to-all-start.3 = ((bf16[8,192,1024]{2,1,0:T(8,128)(2,1)}), bf16[8,192,1024]{2,1,0:T(8,128)(2,1)}, u32[]{:S(2)}, u32[]{:S(2)}) async-start(bf16[8,192,1024]{2,1,0:T(8,128)(2,1)} %bitcast.97), calls=%async_computation.4 | async-start | bytes 6291456 | tf_op jit(solution)/shard_map/all_to_all | solution.py:112
  449.4 8.5 %copy-start.4 = (bf16[8,192,1024]{2,1,0:T(8,128)(2,1)S(1)}, bf16[8,192,1024]{2,1,0:T(8,128)(2,1)}, u32[]{:S(2)}) copy-start(bf16[8,192,1024]{2,1,0:T(8,128)(2,1)} %copy-done.3) | copy-start | bytes 9437188
  449.4 8.5 %copy-start.10 = (bf16[1024,2,8,96]{0,3,2,1:T(8,128)(2,1)S(1)}, bf16[1024,2,8,96]{0,3,2,1:T(8,128)(2,1)}, u32[]{:S(2)}) copy-start(bf16[1024,2,8,96]{0,3,2,1:T(8,128)(2,1)} %all-gather.8.cloned.1.call-done) | copy-start | bytes 9437188
  457.9 5.0 copy-start.11
  518.6 9.4 %copy-start.1 = (bf16[128,1024]{1,0:T(8,128)(2,1)S(1)}, bf16[128,1024]{1,0:T(8,128)(2,1)}, u32[]{:S(2)}) copy-start(bf16[128,1024]{1,0:T(8,128)(2,1)} %param.7) | copy-start | bytes 786436
Sparse Core Ops, SparseCore 0:
  135.2 153.8 all-gather.3
  292.2 37.7 reduce-scatter.1
  333.6 28.8 all-gather.7
  364.0 28.8 all-gather.5
